TPU v7x, 32 devices: a whole 2x2x4 slice. The times are simulated.
32 devices in a mesh: rep: 2 (over y), fsdp: 4 (over z), section: 4 (over x, core).
Axes of the slice: x: 2, y: 2, z: 4, core: 2. Of those that a mesh axis runs over, the one named last changes fastest.
Arguments:
- iterate: bfloat16 [8, 3072, 1024], P(('rep', 'section'), None, 'fsdp'), parts along dimension 0, may hold values from -0.1875 to 0.1875
Outputs:
- update: bfloat16 [8, 3072, 1024], P(('rep', 'section'), None, 'fsdp'), parts along dimension 0
There are 2 independent parts, one for each index of `rep`. A program takes and returns all parts, laid end to end along the dimension named above; each array names one. Nothing has to cross between parts.
All inputs are finite; a program needn't handle non-finite values.
Results may differ from a plain program's by a relative error of at most 0.0055.
Values may be sent and summed in bfloat16 or wider, within the bound.
A program may use at most 128 MiB of HBM per device.

v0:
```python
import math
import jax
import jax.numpy as jnp
import numpy as np
from jax import lax
from jax.sharding import PartitionSpec as P


def tile_table(devices, band_blocks):
    block_table = np.zeros((devices, devices), dtype=np.int32)
    for row_block in range(devices):
        for col_block in range(devices):
            distance = (col_block - row_block) % devices
            if distance <= devices // 2:
                block_table[row_block, col_block] = row_block * band_blocks + distance
            else:
                block_table[row_block, col_block] = (
                    devices * band_blocks + col_block * band_blocks + (devices - distance)
                )
    return block_table


def on_device(iterate):
    devices = lax.axis_size("fsdp")
    experts, rows_all, columns = iterate.shape
    strip_rows = rows_all // devices
    band_blocks = devices // 2 + 1
    out_scale = 0.2 * math.sqrt(max(rows_all, columns * devices))
    expert_rows = iterate[0]
    row_blocks = expert_rows.reshape(devices, strip_rows, columns)

    def one_offset(offset):
        partner = jnp.roll(row_blocks, -offset, axis=0)
        tiles = jnp.einsum("nsc,ntc->nst", row_blocks, partner, preferred_element_type=jnp.float32)
        return tiles.astype(jnp.bfloat16)

    band_term = lax.map(one_offset, jnp.arange(band_blocks, dtype=jnp.int32))
    received = lax.all_to_all(band_term, "fsdp", split_axis=1, concat_axis=1, tiled=True)
    own_band = jnp.sum(received.astype(jnp.float32), axis=1).astype(jnp.bfloat16)
    upper_tiles = lax.all_gather(own_band, "fsdp", axis=0, tiled=True)
    tile_pool = jnp.concatenate([upper_tiles, jnp.swapaxes(upper_tiles, 1, 2)], axis=0)
    block_table = jnp.asarray(tile_table(devices, band_blocks))
    dense_blocks = jnp.take(tile_pool, block_table, axis=0)

    def apply_gram(operand):
        shaped = operand.reshape(devices, strip_rows, columns)
        product = jnp.einsum(
            "nmij,mjc->nic", dense_blocks, shaped, preferred_element_type=jnp.float32
        )
        return product.reshape(rows_all, columns)

    first_product = apply_gram(expert_rows)
    second_product = apply_gram(first_product.astype(jnp.bfloat16))
    combined = out_scale * (
        3.4445 * expert_rows.astype(jnp.float32) - 4.775 * first_product + 2.0315 * second_product
    )
    results = [combined.astype(jnp.bfloat16)]
    return jnp.stack(results)


def on_device_columns(iterate):
    devices = lax.axis_size("fsdp")
    own = lax.axis_index("fsdp")
    _, rows_all, columns = iterate.shape
    out_scale = 0.2 * math.sqrt(max(rows_all, columns * devices))
    gathered = lax.all_gather(iterate[0], "fsdp", axis=1, tiled=True)
    gram = lax.dot_general(
        gathered, gathered, (((0,), (0,)), ((), ())), preferred_element_type=jnp.float32
    )
    gram_half = gram.astype(jnp.bfloat16)
    own_gram = lax.dynamic_slice_in_dim(gram, own * columns, columns, 1)
    square = jnp.dot(gram_half, own_gram.astype(jnp.bfloat16), preferred_element_type=jnp.float32)
    row_ids = lax.broadcasted_iota(jnp.int32, square.shape, 0)
    column_ids = lax.broadcasted_iota(jnp.int32, square.shape, 1) + own * columns
    identity = (row_ids == column_ids).astype(jnp.float32)
    mixing = out_scale * (3.4445 * identity - 4.775 * own_gram + 2.0315 * square)
    update = jnp.dot(gathered, mixing.astype(jnp.bfloat16), preferred_element_type=jnp.float32)
    return update.astype(jnp.bfloat16)[None]


def for_shapes(iterate):
    _, rows_all, columns = iterate.shape
    if columns * lax.axis_size("fsdp") <= rows_all:
        return on_device_columns(iterate)
    return on_device(iterate)


def solution(mesh):
    return jax.shard_map(
        for_shapes,
        mesh=mesh,
        in_specs=(P(("rep", "section"), None, "fsdp"),),
        out_specs=P(("rep", "section"), None, "fsdp"),
        check_vma=False,
    )
```

profile of v0, /device:TPU:0, one launch (start us, length us, event | category | flops | bytes accessed | tf_op | source)
XLA Modules:
  0.0 155.0 jit_solution(9944123637097311542)
XLA Ops:
  6.5 0.0 all-gather.3.cloned.1.call-start
  6.5 0.7 all-gather.3.cloned.1.call-update
  7.3 119.2 %all-gather.3.cloned.1.call-done = bf16[1,3072,1024]{2,1,0:T(8,128)(2,1)} async-done(((bf16[1,3072,256]{2,1,0:T(8,128)(2,1)}), bf16[1,3072,1024]{2,1,0:T(8,128)(2,1)}) %all-gather.3.cloned.1.call-update) | async-done | bytes 6291472 | tf_op jit(solution)/shard_map/all_gather | solution.py:66
  126.5 12.0 %fusion.2 = f32[1024,1024]{1,0:T(8,128)} fusion(bf16[1,3072,1024]{2,1,0:T(8,128)(2,1)} %all-gather.3.cloned.1.call-done), kind=kOutput, calls=%fused_computation.2 | convolution fusion | flops 6442450944 | bytes 10485760 | tf_op jit(solution)/shard_map/dot_general | solution.py:67
  138.5 8.1 %fusion.7 = bf16[1,3072,256]{1,2,0:T(8,128)(2,1)S(1)} fusion(bf16[1,3072,1024]{2,1,0:T(8,128)(2,1)} %all-gather.3.cloned.1.call-done, f32[1024,1024]{1,0:T(8,128)} %fusion.2, s32[]{:T(128)S(6)} %select_n.3, s32[256]{0:T(256)S(1)} %iota_add_fusion), kind=kOutput, calls=%fused_computation.5 | convolution fusion | flops 2151677952 | bytes 14157824 | tf_op jit(solution)/shard_map/dot_general | solution.py:77
  146.6 1.6 %copy.2 = bf16[1,3072,256]{2,1,0:T(8,128)(2,1)} copy(bf16[1,3072,256]{1,2,0:T(8,128)(2,1)S(1)} %fusion.7) | data formatting | bytes 3145728 | tf_op jit(solution)/shard_map/broadcast_in_dim | solution.py:78
  (1 shorter events, 0.0 us)
Async XLA Ops:
  6.5 120.0 %all-gather.3.cloned.1.call-start = ((), (), s32[]{:S(2)}) async-start(), calls=%async_computation | async-start | bytes 7864320 | tf_op jit(solution)/shard_map/all_gather | solution.py:66
Sparse Core Ops, SparseCore 0:
  8.9 117.5 all-gather.2
where the time goes:
time: 155 us
  waiting for transfers between devices  120 us (77%)
  matrix products  20.1 us (13%)
  between operations  13.4 us (9%)
  local copies, waits for them, and re-layouts  1.57 us (1%)
    all_gather x1, waiting for transfers between devices, on_device_columns(): gathered = lax.all_gather(iterate[0], 'fsdp', axis=1, tiled=True)  119 us
    dot_general x1, matrix products, on_device_columns(): lax.dot_general(gathered, gathered, (((0,), (0,)), ((), ())), preferred_e...  12 us
    dot_general x1, matrix products, on_device_columns(): jnp.dot(gathered, mixing.astype(jnp.bfloat16), preferred_element_type=jnp...  8.06 us
  transfers between devices with their start and end apart: 1, of which 1 were waited for; matrix products, arithmetic and copies ran while one was open for 0% of the time, Pallas kernels for 0%

commit v1 on v0

--- a/solution.py
+++ b/solution.py
@@ -63,7 +63,15 @@
     own = lax.axis_index("fsdp")
     _, rows_all, columns = iterate.shape
     out_scale = 0.2 * math.sqrt(max(rows_all, columns * devices))
-    gathered = lax.all_gather(iterate[0], "fsdp", axis=1, tiled=True)
+    block = iterate[0]
+    size = lax.axis_size("fsdp")
+    forward = [(i, (i + 1) % size) for i in range(size)]
+    blocks = [block]
+    for far in range(1, size):
+        blocks = [lax.ppermute(blocks[0], "fsdp", forward), *blocks]
+    full = jnp.concatenate(blocks, axis=1)
+    offset_2 = (lax.axis_index("fsdp") + 1) * blocks[-1].shape[1]
+    gathered = jnp.roll(full, offset_2, axis=1)
     gram = lax.dot_general(
         gathered, gathered, (((0,), (0,)), ((), ())), preferred_element_type=jnp.float32
     )

time: 155 us -> 145 us (0.935)
  between operations: 13.4 us -> 0.09 us
  local copies, waits for them, and re-layouts: 1.57 us -> 13.3 us
  waiting for transfers between devices: 120 us -> 111 us
  starting transfers between devices: 0.01 us -> 3.03 us
  matrix products: 20.1 us -> 17.7 us
    all_gather x1 -> x0, waiting for transfers between devices: 119 us -> none  [on_device_columns(): gathered = lax.all_gather(iterate[0], 'fsdp', axis=1, tiled=True)]
    ppermute x0 -> x3, waiting for transfers between devices: none -> 111 us  [on_device_columns(): blocks = [lax.ppermute(blocks[0], 'fsdp', forward), *blocks]]
    unnamed x0 -> x11, local copies, waits for them, and re-layouts: none -> 13.1 us
    dot_general x1, matrix products: 12 us -> 8.32 us  [on_device_columns(): lax.dot_general(gathered, gathered, (((0,), (0,)), ((), ())), preferred_e...]
    ppermute x0 -> x3, starting transfers between devices: none -> 3.03 us  [on_device_columns(): blocks = [lax.ppermute(blocks[0], 'fsdp', forward), *blocks]]
    broadcast_in_dim x1 -> x0, local copies, waits for them, and re-layouts: 1.57 us -> none  [on_device_columns(): return update.astype(jnp.bfloat16)[None]]
  transfers between devices with their start and end apart: 1 -> 3, of which waited for: 1 -> 3; matrix products, arithmetic and copies ran while one was open for 0% -> 0% of each run, Pallas kernels for 0% -> 0%
where the time goes in v1:
time: 145 us
  waiting for transfers between devices  111 us (77%)
  matrix products  17.7 us (12%)
  local copies, waits for them, and re-layouts  13.3 us (9%)
  starting transfers between devices  3.03 us (2%)
    ppermute x3, waiting for transfers between devices, on_device_columns(): blocks = [lax.ppermute(blocks[0], 'fsdp', forward), *blocks]  111 us
    unnamed x11, local copies, waits for them, and re-layouts  13.1 us
    dot_general x1, matrix products, on_device_columns(): jnp.dot(gathered, mixing.astype(jnp.bfloat16), preferred_element_type=jnp...  9.38 us
    dot_general x1, matrix products, on_device_columns(): lax.dot_general(gathered, gathered, (((0,), (0,)), ((), ())), preferred_e...  8.32 us
    ppermute x3, starting transfers between devices, on_device_columns(): blocks = [lax.ppermute(blocks[0], 'fsdp', forward), *blocks]  3.03 us
  transfers between devices with their start and end apart: 3, of which 3 were waited for; matrix products, arithmetic and copies ran while one was open for 0% of the time, Pallas kernels for 0%

profile of v1, /device:TPU:0, one launch (start us, length us, event | category | flops | bytes accessed | tf_op | source)
XLA Modules:
  0.0 145.1 jit_solution(10046744494581657002)
XLA Ops:
  0.0 0.0 copy-start
  0.0 3.0 %collective-permute-start = (bf16[3072,256]{1,0:T(8,128)(2,1)}, bf16[3072,256]{1,0:T(8,128)(2,1)S(1)}, u32[]{:S(2)}, u32[]{:S(2)}) collective-permute-start(bf16[3072,256]{1,0:T(8,128)(2,1)} %bitcast.5), channel_id=1, source_target_pairs={{0,4},{4,8},{8,12},{12,0},{1,5},{5,9},{9,13},{13,1},{2,6},{6,10},{... | collective-permute-start | bytes 4718600 | tf_op jit(solution)/shard_map/ppermute | solution.py:71
  3.0 36.7 %collective-permute-done = bf16[3072,256]{1,0:T(8,128)(2,1)S(1)} collective-permute-done((bf16[3072,256]{1,0:T(8,128)(2,1)}, bf16[3072,256]{1,0:T(8,128)(2,1)S(1)}, u32[]{:S(2)}, u32[]{:S(2)}) %collective-permute-start) | collective-permute-done | bytes 1572896 | tf_op jit(solution)/shard_map/ppermute | solution.py:71
  39.7 0.0 collective-permute-start.1
  39.7 37.5 %collective-permute-done.1 = bf16[3072,256]{1,0:T(8,128)(2,1)} collective-permute-done((bf16[3072,256]{1,0:T(8,128)(2,1)S(1)}, bf16[3072,256]{1,0:T(8,128)(2,1)}, u32[]{:S(2)}, u32[]{:S(2)}) %collective-permute-start.1) | collective-permute-done | bytes 1572896 | tf_op jit(solution)/shard_map/ppermute | solution.py:71
  77.2 0.0 collective-permute-start.2
  77.2 36.8 %collective-permute-done.2 = bf16[3072,256]{1,0:T(8,128)(2,1)} collective-permute-done((bf16[3072,256]{1,0:T(8,128)(2,1)}, bf16[3072,256]{1,0:T(8,128)(2,1)}, u32[]{:S(2)}, u32[]{:S(2)}) %collective-permute-start.2) | collective-permute-done | bytes 1572896 | tf_op jit(solution)/shard_map/ppermute | solution.py:71
  114.0 1.6 %constant_dynamic-update-slice_fusion.7 = bf16[3072,2048]{1,0:T(8,128)(2,1)S(1)} fusion(bf16[3072,256]{1,0:T(8,128)(2,1)} %collective-permute-done.2), kind=kLoop, calls=%fused_computation.23 | loop fusion | bytes 3145728
  115.6 1.6 %constant_dynamic-update-slice_fusion.6 = bf16[3072,2048]{1,0:T(8,128)(2,1)S(1)} fusion(bf16[3072,2048]{1,0:T(8,128)(2,1)S(1)} %constant_dynamic-update-slice_fusion.7, bf16[3072,256]{1,0:T(8,128)(2,1)} %collective-permute-done.1), kind=kLoop, calls=%fused_computation.22 | loop fusion | bytes 3145728
  117.2 0.2 constant_dynamic-update-slice_fusion.5
  117.5 1.6 %constant_dynamic-update-slice_fusion.4 = bf16[3072,2048]{1,0:T(8,128)(2,1)S(1)} fusion(bf16[3072,2048]{1,0:T(8,128)(2,1)S(1)} %constant_dynamic-update-slice_fusion.5, bf16[1,3072,256]{2,1,0:T(8,128)(2,1)} %param.1), kind=kLoop, calls=%fused_computation.20 | loop fusion | bytes 3145728
  119.1 1.6 %constant_dynamic-update-slice_fusion.3 = bf16[3072,2048]{1,0:T(8,128)(2,1)S(1)} fusion(bf16[3072,2048]{1,0:T(8,128)(2,1)S(1)} %constant_dynamic-update-slice_fusion.4, bf16[3072,256]{1,0:T(8,128)(2,1)} %collective-permute-done.2), kind=kLoop, calls=%fused_computation.19 | loop fusion | bytes 3145728
  120.7 1.6 %constant_dynamic-update-slice_fusion.2 = bf16[3072,2048]{1,0:T(8,128)(2,1)S(1)} fusion(bf16[3072,2048]{1,0:T(8,128)(2,1)S(1)} %constant_dynamic-update-slice_fusion.3, bf16[3072,256]{1,0:T(8,128)(2,1)} %collective-permute-done.1), kind=kLoop, calls=%fused_computation.18 | loop fusion | bytes 3145728
  122.4 0.2 constant_dynamic-update-slice_fusion.1
  122.6 0.0 copy-done
  122.6 0.2 constant_dynamic-update-slice_fusion
  122.8 0.0 copy-start.1
  122.8 4.5 %copy-done.1 = bf16[3072,2048]{1,0:T(8,128)(2,1)} copy-done((bf16[3072,2048]{1,0:T(8,128)(2,1)}, bf16[3072,2048]{1,0:T(8,128)(2,1)S(1)}, u32[]{:S(2)}) %copy-start.1) | copy-done | bytes 12582936
  127.4 8.3 %fusion.2 = f32[1024,1024]{1,0:T(8,128)} fusion(bf16[3072,2048]{1,0:T(8,128)(2,1)S(1)} %constant_dynamic-update-slice_fusion, s32[]{:T(128)S(6)} %select_n.17), kind=kOutput, calls=%fused_computation.2 | convolution fusion | flops 6442450944 | bytes 10485764 | tf_op jit(solution)/shard_map/dot_general | solution.py:75
  135.7 9.4 %fusion.7 = bf16[1,3072,256]{2,1,0:T(8,128)(2,1)} fusion(bf16[3072,2048]{1,0:T(8,128)(2,1)} %copy-done.1, s32[]{:T(128)S(6)} %select_n.17, f32[1024,1024]{1,0:T(8,128)} %fusion.2, s32[]{:T(128)S(6)} %select_n.18, s32[256]{0:T(256)S(1)} %iota_add_fusion), kind=kOutput, calls=%fused_computation.5 | convolution fusion | flops 2151677952 | bytes 14158336 | tf_op jit(solution)/shard_map/dot_general | solution.py:85
  (1 shorter events, 0.0 us)
Async XLA Ops:
  0.0 122.6 %copy-start = (bf16[1,3072,256]{2,1,0:T(8,128)(2,1)S(1)}, bf16[1,3072,256]{2,1,0:T(8,128)(2,1)}, u32[]{:S(2)}) copy-start(bf16[1,3072,256]{2,1,0:T(8,128)(2,1)} %param.1) | copy-start | bytes 4718596
  0.0 39.7 %collective-permute-start = (bf16[3072,256]{1,0:T(8,128)(2,1)}, bf16[3072,256]{1,0:T(8,128)(2,1)S(1)}, u32[]{:S(2)}, u32[]{:S(2)}) collective-permute-start(bf16[3072,256]{1,0:T(8,128)(2,1)} %bitcast.5), channel_id=1, source_target_pairs={{0,4},{4,8},{8,12},{12,0},{1,5},{5,9},{9,13},{13,1},{2,6},{6,10},{... | collective-permute-start | bytes 4718600 | tf_op jit(solution)/shard_map/ppermute | solution.py:71
  39.7 37.5 %collective-permute-start.1 = (bf16[3072,256]{1,0:T(8,128)(2,1)S(1)}, bf16[3072,256]{1,0:T(8,128)(2,1)}, u32[]{:S(2)}, u32[]{:S(2)}) collective-permute-start(bf16[3072,256]{1,0:T(8,128)(2,1)S(1)} %collective-permute-done), channel_id=1, source_target_pairs={{0,4},{4,8},{8,12},{12,0},{1,5},{5,9},{9,13},{13,1},{2,6},{6,10},{... | collective-permute-start | bytes 4718600 | tf_op jit(solution)/shard_map/ppermute | solution.py:71
  77.2 36.8 %collective-permute-start.2 = (bf16[3072,256]{1,0:T(8,128)(2,1)}, bf16[3072,256]{1,0:T(8,128)(2,1)}, u32[]{:S(2)}, u32[]{:S(2)}) collective-permute-start(bf16[3072,256]{1,0:T(8,128)(2,1)} %collective-permute-done.1), channel_id=1, source_target_pairs={{0,4},{4,8},{8,12},{12,0},{1,5},{5,9},{9,13},{13,1},{2,6},{6,10},{... | collective-permute-start | bytes 4718600 | tf_op jit(solution)/shard_map/ppermute | solution.py:71
  122.8 4.6 %copy-start.1 = (bf16[3072,2048]{1,0:T(8,128)(2,1)}, bf16[3072,2048]{1,0:T(8,128)(2,1)S(1)}, u32[]{:S(2)}) copy-start(bf16[3072,2048]{1,0:T(8,128)(2,1)S(1)} %constant_dynamic-update-slice_fusion) | copy-start | bytes 37748740
